TPU v7x, 128 devices: a whole 4x4x4 slice. The times are simulated.
128 devices in a mesh: pts: 32 (over z, x, core), rep: 4 (over y).
Axes of the slice: x: 4, y: 4, z: 4, core: 2. Of those that a mesh axis runs over, the one named last changes fastest.
Arguments:
- target_xyz: float32 [3, 32768], P(None, 'pts'), may hold values from 0 to 1
- source_xyz: float32 [3, 65536], P(None, ('pts', 'rep')), may hold values from 0 to 1
- target_count: int32 [32], P('pts'), may hold values from 1 to 1024, as said below
- source_count: int32 [128], P(('pts', 'rep')), may hold values from 1 to 512, as said below
- psi: bfloat16 [32768, 256], P('pts'), may hold values from -6 to 6
- omega: bfloat16 [65536, 256], P(('pts', 'rep')), may hold values from -6 to 6
Outputs:
- range_sketch: float32 [32768, 256], P('pts')
- corange_sketch: float32 [65536, 256], P(('pts', 'rep'))
- core: float32 [256, 256], replicated
- range_gram: float32 [256, 256], replicated
- corange_gram: float32 [256, 256], replicated
Inputs may be any that keep to these rules, and one draw needn't show every extreme that they name: `target_count`: each group holds 1 to 1024 live targets; some group holds exactly 1024. `source_count`: each shard holds 1 to 512 live sources; some shard holds exactly 512.
All inputs are finite; a program needn't handle non-finite values.
Results may differ from a plain program's by a relative error of at most 0.0003.
The roundings to bfloat16 on the way count: a program that leaves them out, or rounds other values in their place, can miss the bound.
Values may be sent and summed in bfloat16 or wider, within the bound.
No kernel may reach another device: no remote copies, remote signals or barrier semaphores. Data moves between devices by JAX's collectives and lax.ppermute only.
A program may use at most 64 MiB of HBM per device.

v0:
```python
import math
import jax
import jax.numpy as jnp
from jax import lax
from jax.sharding import PartitionSpec as P

SHIFT = 1.05
SPREAD = 8.0


def tile_block(tgt, src):
    dx = tgt[0][:, None] - (src[0][None, :] + SHIFT)
    dy = SPREAD * (tgt[1][:, None] - src[1][None, :])
    dz = SPREAD * (tgt[2][:, None] - src[2][None, :])
    return lax.rsqrt(dx * dx + dy * dy + dz * dz).astype(jnp.bfloat16)


def local(target_xyz, source_xyz, target_count, source_count, psi, omega):
    tcap = psi.shape[0]
    scap = omega.shape[0]
    width = psi.shape[1]
    n_pts = lax.axis_size("pts")
    n_rep = lax.axis_size("rep")
    all_targets = tcap * n_pts
    all_sources = scap * n_pts * n_rep
    tlive = jnp.arange(tcap, dtype=jnp.int32) < target_count[0]
    slive = jnp.arange(scap, dtype=jnp.int32) < source_count[0]
    psi_live = jnp.where(tlive[:, None], psi, jnp.zeros_like(psi))
    omega_live = jnp.where(slive[:, None], omega, jnp.zeros_like(omega))
    hi = lax.Precision.HIGHEST
    src_all = lax.all_gather(source_xyz, "pts", axis=1, tiled=True)
    piece = lax.all_gather(omega_live, "pts", axis=0, tiled=True)

    def range_inner(j, acc):
        rows = lax.dynamic_slice_in_dim(piece, j * scap, scap, 0)
        where = lax.dynamic_slice_in_dim(src_all, j * scap, scap, 1)
        return acc + jnp.dot(
            tile_block(target_xyz, where), rows, preferred_element_type=jnp.float32
        )

    y_part = lax.fori_loop(
        0, piece.shape[0] // scap, range_inner, jnp.zeros((tcap, width), jnp.float32)
    )
    y_sum = lax.psum(y_part, "rep") * (2.0 / math.sqrt(all_sources))
    range_sketch = jnp.where(tlive[:, None], y_sum, jnp.zeros_like(y_sum))
    tgt_all = lax.all_gather(target_xyz, "pts", axis=1, tiled=True)
    corange_piece = lax.all_gather(psi_live, "pts", axis=0, tiled=True)

    def corange_inner(j, acc):
        rows = lax.dynamic_slice_in_dim(corange_piece, j * tcap, tcap, 0)
        where = lax.dynamic_slice_in_dim(tgt_all, j * tcap, tcap, 1)
        tile = tile_block(where, source_xyz)
        return acc + lax.dot_general(
            tile, rows, (((0,), (0,)), ((), ())), preferred_element_type=jnp.float32
        )

    z_sum = lax.fori_loop(
        0, corange_piece.shape[0] // tcap, corange_inner, jnp.zeros((scap, width), jnp.float32)
    )
    z_scaled = z_sum * (2.0 / math.sqrt(all_targets))
    corange_sketch = jnp.where(slive[:, None], z_scaled, jnp.zeros_like(z_scaled))
    z_gram_part = jnp.dot(corange_sketch.T, corange_sketch, precision=hi)
    core_part = jnp.dot(psi_live.astype(jnp.float32).T, range_sketch, precision=hi)
    y_gram_part = jnp.dot(range_sketch.T, range_sketch, precision=hi)
    core_sum, y_gram = lax.psum((core_part, y_gram_part), "pts")
    z_gram = lax.psum(z_gram_part, ("pts", "rep"))
    core = core_sum / math.sqrt(all_targets)
    range_gram = y_gram / all_targets
    corange_gram = z_gram / all_sources
    return (range_sketch, corange_sketch, core, range_gram, corange_gram)


def solution(mesh):
    return jax.shard_map(
        local,
        mesh=mesh,
        in_specs=(
            P(None, "pts"),
            P(None, ("pts", "rep")),
            P("pts"),
            P(("pts", "rep")),
            P("pts", None),
            P(("pts", "rep"), None),
        ),
        out_specs=(P("pts", None), P(("pts", "rep"), None), P(), P(), P()),
        check_vma=False,
    )
```

profile of v0, /device:TPU:1, one launch (start us, length us, event | category | flops | bytes accessed | tf_op | source)
XLA Modules:
  0.0 550.0 jit_solution(14603858195827019406)
XLA Ops:
  9.7 27.6 %all_gather.12 = f32[3,16384]{1,0:T(4,128)S(1)} all-gather(f32[3,512]{1,0:T(4,128)} %param.11), channel_id=1, replica_groups=mesh['pts'=32,'rep'=4] {'pts'}, dimensions={1}, use_global_device_ids=true | all-gather | bytes 202752 | tf_op jit(solution)/shard_map/all_gather | solution.py:31
  37.3 30.2 %all-gather.3.cloned.1.call-done = bf16[16384,256]{1,0:T(8,128)(2,1)} async-done(((bf16[512,256]{1,0:T(8,128)(2,1)}), bf16[16384,256]{1,0:T(8,128)(2,1)}) %all-gather.3.cloned.1.call-update) | async-done | bytes 8388624 | tf_op jit(solution)/shard_map/all_gather | solution.py:32
  67.5 96.4 %while.28 = (s32[]{:T(128)}, f32[1024,256]{1,0:T(8,128)S(1)}, f32[3,1024]{1,0:T(4,128)}, f32[3,16384]{1,0:T(4,128)S(1)}, bf16[16384,256]{1,0:T(8,128)(2,1)}, /*i...) while((s32[]{:T(128)}, f32[1024,256]{1,0:T(8,128)S(1)}, ...), condition=%wide.region_1.2_spmd.clone, body=%wide.region_0.1_spmd.clone.sunk | while | flops 274727424 | bytes 2414797 | solution.py:41
  68.4 2.0 convolution_add_fusion.4
  83.5 2.0 convolution_add_fusion.4
  86.5 2.0 convolution_add_fusion.4
  119.6 2.0 convolution_add_fusion.4
  122.7 2.0 convolution_add_fusion.4
  134.7 2.0 convolution_add_fusion.4
  166.7 24.7 %all_gather.14 = f32[3,32768]{1,0:T(4,128)S(1)} all-gather(f32[3,1024]{1,0:T(4,128)S(1)} %copy-done.5), channel_id=1, replica_groups=mesh['pts'=32,'rep'=4] {'pts'}, dimensions={1}, use_global_device_ids=true | all-gather | bytes 405504 | tf_op jit(solution)/shard_map/all_gather | solution.py:46
  191.4 17.0 %all-reduce.5.cloned.1.call-done = f32[1024,256]{1,0:T(8,128)} async-done(((f32[1024,256]{1,0:T(8,128)}), f32[1024,256]{1,0:T(8,128)}) %all-reduce.5.cloned.1.call-update) | async-done | bytes 1048592 | tf_op jit(solution)/shard_map/psum | solution.py:44
  211.4 2.6 fusion.22
  214.0 73.1 %all-gather.5.cloned.1.call-done = bf16[32768,256]{1,0:T(8,128)(2,1)} async-done(((bf16[1024,256]{1,0:T(8,128)(2,1)}), bf16[32768,256]{1,0:T(8,128)(2,1)}) %all-gather.5.cloned.1.call-update) | async-done | bytes 16777232 | tf_op jit(solution)/shard_map/all_gather | solution.py:47
  287.1 81.4 %while.29 = (s32[]{:T(128)}, f32[512,256]{1,0:T(8,128)S(1)}, f32[3,32768]{1,0:T(4,128)S(1)}, f32[3,512]{1,0:T(4,128)S(1)}, bf16[32768,256]{1,0:T(8,128)(2,1)}, /...) while((s32[]{:T(128)}, f32[512,256]{1,0:T(8,128)S(1)}, ...), condition=%wide.region_4.5_spmd.clone, body=%wide.region_3.4_spmd.clone.sunk | while | flops 274465280 | bytes 1628365 | solution.py:57
  287.2 2.4 convolution_add_fusion.5
  289.8 2.4 convolution_add_fusion.5
  292.3 2.4 convolution_add_fusion.5
  294.8 2.4 convolution_add_fusion.5
  297.4 2.4 convolution_add_fusion.5
  300.0 2.4 convolution_add_fusion.5
  302.5 2.4 convolution_add_fusion.5
  305.0 2.4 convolution_add_fusion.5
  307.6 2.4 convolution_add_fusion.5
  310.1 2.4 convolution_add_fusion.5
  312.7 2.4 convolution_add_fusion.5
  315.2 2.4 convolution_add_fusion.5
  317.8 2.4 convolution_add_fusion.5
  320.3 2.4 convolution_add_fusion.5
  322.9 2.4 convolution_add_fusion.5
  325.4 2.4 convolution_add_fusion.5
  327.9 2.4 convolution_add_fusion.5
  330.5 2.4 convolution_add_fusion.5
  333.0 2.4 convolution_add_fusion.5
  335.6 2.4 convolution_add_fusion.5
  338.1 2.4 convolution_add_fusion.5
  340.7 2.4 convolution_add_fusion.5
  343.2 2.4 convolution_add_fusion.5
  345.8 2.4 convolution_add_fusion.5
  348.3 2.4 convolution_add_fusion.5
  350.9 2.4 convolution_add_fusion.5
  353.4 2.4 convolution_add_fusion.5
  355.9 2.4 convolution_add_fusion.5
  358.5 2.4 convolution_add_fusion.5
  361.0 2.4 convolution_add_fusion.5
  363.6 2.4 convolution_add_fusion.5
  366.1 2.4 convolution_add_fusion.5
  370.5 24.1 %all-reduce.9.cloned.1.call-done = (f32[256,256]{1,0:T(8,128)}, f32[256,256]{1,0:T(8,128)}) async-done(((f32[256,256]{1,0:T(8,128)}, f32[256,256]{1,0:T(8,128)}), (f32[256,256]{1,0:T(8,128)}, f32[256,256]{1,0:T(8,128)})) %all-reduce.9.cloned.1.call-update) | async-done | bytes 524304 | tf_op jit(solution)/shard_map/psum | solution.py:65
  396.4 145.4 %all-reduce.7.cloned.1.call-done = f32[256,256]{1,0:T(8,128)} async-done(((f32[256,256]{1,0:T(8,128)}), f32[256,256]{1,0:T(8,128)}) %all-reduce.7.cloned.1.call-update) | async-done | bytes 262160 | tf_op jit(solution)/shard_map/psum | solution.py:66
  (190 shorter events, 98.5 us)
Async XLA Ops:
  7.2 60.3 %all-gather.3.cloned.1.call-start = ((), (), s32[]{:S(2)}) async-start(), calls=%async_computation | async-start | bytes 8650752 | tf_op jit(solution)/shard_map/all_gather | solution.py:32
  9.7 198.7 %all-reduce.5.cloned.1.call-start = ((), (), s32[]{:S(2)}) async-start(), calls=%async_computation.1 | async-start | bytes 2097152 | tf_op jit(solution)/shard_map/psum | solution.py:44
  67.5 98.1 %copy-start.4 = (bf16[1024,256]{1,0:T(8,128)(2,1)S(1)}, bf16[1024,256]{1,0:T(8,128)(2,1)}, u32[]{:S(2)}) copy-start(bf16[1024,256]{1,0:T(8,128)(2,1)} %param.14) | copy-start | bytes 1572868
  163.9 1.0 copy-start.3
  163.9 2.8 copy-start.5
  164.9 122.2 %all-gather.5.cloned.1.call-start = ((), (), s32[]{:S(2)}) async-start(), calls=%async_computation.2 | async-start | bytes 17301504 | tf_op jit(solution)/shard_map/all_gather | solution.py:47
  166.6 43.2 %copy-start.2 = (bf16[1024,256]{1,0:T(8,128)(2,1)S(1)}, bf16[1024,256]{1,0:T(8,128)(2,1)}, u32[]{:S(2)}) copy-start(bf16[1024,256]{1,0:T(8,128)(2,1)} %broadcast_select_fusion) | copy-start | bytes 1572868
  166.6 227.9 %all-reduce.9.cloned.1.call-start = ((), (), s32[]{:S(2)}) async-start(), calls=%async_computation.4 | async-start | bytes 1048576 | tf_op jit(solution)/shard_map/psum | solution.py:65
  209.8 4.1 copy-start
  209.9 77.3 %copy-start.6 = (f32[3,512]{1,0:T(4,128)S(1)}, f32[3,512]{1,0:T(4,128)}, u32[]{:S(2)}) copy-start(f32[3,512]{1,0:T(4,128)} %param.11) | copy-start | bytes 18436
  214.0 327.8 %all-reduce.7.cloned.1.call-start = ((), (), s32[]{:S(2)}) async-start(), calls=%async_computation.3 | async-start | bytes 524288 | tf_op jit(solution)/shard_map/psum | solution.py:66
  368.7 174.8 %copy-start.1 = (f32[512,256]{1,0:T(8,128)}, f32[512,256]{1,0:T(8,128)S(1)}, u32[]{:S(2)}) copy-start(f32[512,256]{1,0:T(8,128)S(1)} %multiply_select_fusion.1) | copy-start | bytes 1572868
Sparse Core Ops, SparseCore 0:
  10.8 56.6 all-gather.2
  165.0 43.3 all-reduce.4
  211.2 75.8 all-gather.4
  290.8 103.6 all-reduce.8
  399.1 142.5 all-reduce.6
where the time goes:
time: 555 us; the launch traced here: 550 us
  waiting for transfers between devices  290 us (52%)
  matrix products  148 us (27%)
  blocking collectives  52.2 us (9%)
  local copies, waits for them, and re-layouts  30.9 us (6%)
  between operations  15.2 us (3%)
  other arithmetic  10.8 us (2%)
    psum x1, waiting for transfers between devices, local(): z_gram = lax.psum(z_gram_part, ('pts', 'rep'))  145 us
    dot_general x32, matrix products, corange_inner(): lax.dot_general(tile, rows, (((0,), (0,)), ((), ())), preferred_element_t...  76.9 us
    all_gather x1, waiting for transfers between devices, local(): corange_piece = lax.all_gather(psi_live, 'pts', axis=0, tiled=True)  73.1 us
    dot_general x32, matrix products, range_inner(): jnp.dot(tile_block(target_xyz, where), rows, preferred_element_type=jnp.f...  65.5 us
    all_gather x1, waiting for transfers between devices, local(): piece = lax.all_gather(omega_live, 'pts', axis=0, tiled=True)  30.2 us
    slice x64, local copies, waits for them, and re-layouts, tile_block(): dx = tgt[0][:, None] - (src[0][None, :] + SHIFT)  30 us
    all_gather x1, blocking collectives, local(): src_all = lax.all_gather(source_xyz, 'pts', axis=1, tiled=True)  27.6 us
    all_gather x1, blocking collectives, local(): tgt_all = lax.all_gather(target_xyz, 'pts', axis=1, tiled=True)  24.7 us
  transfers between devices with their start and end apart: 5, of which 5 were waited for; matrix products, arithmetic and copies ran while one was open for 16% of the time, Pallas kernels for 0%

commit v1 on v0

--- a/solution.py
+++ b/solution.py
@@ -44,7 +44,9 @@
     y_sum = lax.psum(y_part, "rep") * (2.0 / math.sqrt(all_sources))
     range_sketch = jnp.where(tlive[:, None], y_sum, jnp.zeros_like(y_sum))
     tgt_all = lax.all_gather(target_xyz, "pts", axis=1, tiled=True)
-    corange_piece = lax.all_gather(psi_live, "pts", axis=0, tiled=True)
+    corange_piece = jnp.concatenate(
+        lax.all_to_all(jnp.stack([psi_live] * lax.axis_size("pts")), "pts", 0, 0), axis=0
+    )
 
     def corange_inner(j, acc):
         rows = lax.dynamic_slice_in_dim(corange_piece, j * tcap, tcap, 0)

time: 555 us -> 710 us (1.28)
  blocking collectives: 52.2 us -> 270 us
  waiting for transfers between devices: 290 us -> 240 us
  local copies, waits for them, and re-layouts: 30.9 us -> 10.2 us
  starting transfers between devices: 0.21 us -> 9.77 us
    all_gather x1, blocking collectives: 27.6 us -> 244 us  [local(): src_all = lax.all_gather(source_xyz, 'pts', axis=1, tiled=True)]
    psum x1, waiting for transfers between devices: 24.1 us -> 104 us  [local(): core_sum, y_gram = lax.psum((core_part, y_gram_part), 'pts')]
    all_gather x1 -> x0, waiting for transfers between devices: 73.1 us -> none  [local(): corange_piece = lax.all_gather(psi_live, 'pts', axis=0, tiled=True)]
    all_gather x1, waiting for transfers between devices: 30.2 us -> 0.01 us  [local(): piece = lax.all_gather(omega_live, 'pts', axis=0, tiled=True)]
    slice x64, local copies, waits for them, and re-layouts: 30 us -> 3.26 us  [tile_block(): dx = tgt[0][:, None] - (src[0][None, :] + SHIFT)]
    psum x1, waiting for transfers between devices: 17 us -> 0.02 us  [local(): y_sum = lax.psum(y_part, 'rep') * (2.0 / math.sqrt(all_sources))]
    psum x1, waiting for transfers between devices: 145 us -> 136 us  [local(): z_gram = lax.psum(z_gram_part, ('pts', 'rep'))]
    all_to_all x0 -> x1, starting transfers between devices: none -> 9.61 us  [local(): lax.all_to_all(jnp.stack([psi_live] * lax.axis_size('pts')), 'pts', 0, 0)]
  transfers between devices with their start and end apart: 5 -> 5, of which waited for: 5 -> 2; matrix products, arithmetic and copies ran while one was open for 16% -> 23% of each run, Pallas kernels for 0% -> 0%
where the time goes in v1:
time: 710 us; the launch traced here: 707 us
  blocking collectives  270 us (38%)
  waiting for transfers between devices  240 us (34%)
  matrix products  148 us (21%)
  between operations  15.2 us (2%)
  other arithmetic  11.1 us (2%)
  local copies, waits for them, and re-layouts  10.2 us (1%)
  starting transfers between devices  9.77 us (1%)
    all_gather x1, blocking collectives, local(): src_all = lax.all_gather(source_xyz, 'pts', axis=1, tiled=True)  244 us
    psum x1, waiting for transfers between devices, local(): z_gram = lax.psum(z_gram_part, ('pts', 'rep'))  136 us
    psum x1, waiting for transfers between devices, local(): core_sum, y_gram = lax.psum((core_part, y_gram_part), 'pts')  104 us
    dot_general x32, matrix products, corange_inner(): lax.dot_general(tile, rows, (((0,), (0,)), ((), ())), preferred_element_t...  76.9 us
    dot_general x32, matrix products, range_inner(): jnp.dot(tile_block(target_xyz, where), rows, preferred_element_type=jnp.f...  65.2 us
    all_gather x1, blocking collectives, local(): tgt_all = lax.all_gather(target_xyz, 'pts', axis=1, tiled=True)  25.6 us
  transfers between devices with their start and end apart: 5, of which 2 were waited for; matrix products, arithmetic and copies ran while one was open for 23% of the time, Pallas kernels for 0%

profile of v1, /device:TPU:1, one launch (start us, length us, event | category | flops | bytes accessed | tf_op | source)
XLA Modules:
  0.0 706.7 jit_solution(6561683813296978070)
XLA Ops:
  11.6 6.0 stack.2
  17.6 9.6 %all-to-all-start = ((bf16[32,1024,256]{2,1,0:T(8,128)(2,1)}), bf16[32,1024,256]{2,1,0:T(8,128)(2,1)}, u32[]{:S(2)}, u32[]{:S(2)}) async-start(bf16[32,1024,256]{2,1,0:T(8,128)(2,1)} %stack.2), calls=%async_computation | async-start | bytes 33554432 | tf_op jit(solution)/shard_map/all_to_all | solution.py:48
  27.3 244.5 %all_gather.9 = f32[3,16384]{1,0:T(4,128)S(1)} all-gather(f32[3,512]{1,0:T(4,128)S(1)} %copy-done.4), channel_id=1, replica_groups=mesh['pts'=32,'rep'=4] {'pts'}, dimensions={1}, use_global_device_ids=true | all-gather | bytes 202752 | tf_op jit(solution)/shard_map/all_gather | solution.py:31
  271.8 25.6 %all_gather.11 = f32[3,32768]{1,0:T(4,128)S(1)} all-gather(f32[3,1024]{1,0:T(4,128)S(1)} %copy-done.3), channel_id=1, replica_groups=mesh['pts'=32,'rep'=4] {'pts'}, dimensions={1}, use_global_device_ids=true | all-gather | bytes 405504 | tf_op jit(solution)/shard_map/all_gather | solution.py:46
  297.4 69.5 %while.28 = (s32[]{:T(128)}, f32[1024,256]{1,0:T(8,128)S(1)}, f32[3,1024]{1,0:T(4,128)S(1)}, f32[3,16384]{1,0:T(4,128)S(1)}, bf16[16384,256]{1,0:T(8,128)(2,1)},...) while((s32[]{:T(128)}, f32[1024,256]{1,0:T(8,128)S(1)}, ...), condition=%wide.region_1.2_spmd.clone, body=%wide.region_0.1_spmd.clone.sunk | while | flops 274727424 | bytes 2414797 | solution.py:41
  314.9 2.0 convolution_add_fusion.4
  317.1 2.0 convolution_add_fusion.4
  319.3 2.0 convolution_add_fusion.4
  321.4 2.0 convolution_add_fusion.4
  341.0 2.0 convolution_add_fusion.4
  343.1 2.0 convolution_add_fusion.4
  345.3 2.0 convolution_add_fusion.4
  368.0 81.4 %while.29 = (s32[]{:T(128)}, f32[512,256]{1,0:T(8,128)S(1)}, f32[3,32768]{1,0:T(4,128)S(1)}, f32[3,512]{1,0:T(4,128)S(1)}, bf16[32768,256]{1,0:T(8,128)(2,1)}, /...) while((s32[]{:T(128)}, f32[512,256]{1,0:T(8,128)S(1)}, ...), condition=%wide.region_4.5_spmd.clone, body=%wide.region_3.4_spmd.clone.sunk | while | flops 274465280 | bytes 1628365 | solution.py:59
  368.1 2.4 convolution_add_fusion.5
  370.6 2.4 convolution_add_fusion.5
  373.2 2.4 convolution_add_fusion.5
  375.7 2.4 convolution_add_fusion.5
  378.3 2.4 convolution_add_fusion.5
  380.8 2.4 convolution_add_fusion.5
  383.4 2.4 convolution_add_fusion.5
  385.9 2.4 convolution_add_fusion.5
  388.5 2.4 convolution_add_fusion.5
  391.0 2.4 convolution_add_fusion.5
  393.5 2.4 convolution_add_fusion.5
  396.1 2.4 convolution_add_fusion.5
  398.6 2.4 convolution_add_fusion.5
  401.2 2.4 convolution_add_fusion.5
  403.7 2.4 convolution_add_fusion.5
  406.3 2.4 convolution_add_fusion.5
  408.8 2.4 convolution_add_fusion.5
  411.4 2.4 convolution_add_fusion.5
  413.9 2.4 convolution_add_fusion.5
  416.5 2.4 convolution_add_fusion.5
  419.0 2.4 convolution_add_fusion.5
  421.6 2.4 convolution_add_fusion.5
  424.1 2.4 convolution_add_fusion.5
  426.6 2.4 convolution_add_fusion.5
  429.2 2.4 convolution_add_fusion.5
  431.7 2.4 convolution_add_fusion.5
  434.3 2.4 convolution_add_fusion.5
  436.8 2.4 convolution_add_fusion.5
  439.4 2.4 convolution_add_fusion.5
  441.9 2.4 convolution_add_fusion.5
  444.4 2.4 convolution_add_fusion.5
  447.0 2.4 convolution_add_fusion.5
  452.8 2.5 fusion.22
  456.9 135.6 %all-reduce.7.cloned.1.call-done = f32[256,256]{1,0:T(8,128)} async-done(((f32[256,256]{1,0:T(8,128)}), f32[256,256]{1,0:T(8,128)}) %all-reduce.7.cloned.1.call-update) | async-done | bytes 262160 | tf_op jit(solution)/shard_map/psum | solution.py:68
  594.2 104.1 %all-reduce.9.cloned.1.call-done = (f32[256,256]{1,0:T(8,128)}, f32[256,256]{1,0:T(8,128)}) async-done(((f32[256,256]{1,0:T(8,128)}, f32[256,256]{1,0:T(8,128)}), (f32[256,256]{1,0:T(8,128)}, f32[256,256]{1,0:T(8,128)})) %all-reduce.9.cloned.1.call-update) | async-done | bytes 524304 | tf_op jit(solution)/shard_map/psum | solution.py:67
  (186 shorter events, 69.7 us)
Async XLA Ops:
  7.2 290.3 %all-gather.2.cloned.1.call-start = ((), (), s32[]{:S(2)}) async-start(), calls=%async_computation.1 | async-start | bytes 8650752 | tf_op jit(solution)/shard_map/all_gather | solution.py:32
  17.6 9.7 %copy-start.4 = (f32[3,512]{1,0:T(4,128)S(1)}, f32[3,512]{1,0:T(4,128)}, u32[]{:S(2)}) copy-start(f32[3,512]{1,0:T(4,128)} %param.11) | copy-start | bytes 18436
  17.6 254.2 %copy-start.3 = (f32[3,1024]{1,0:T(4,128)S(1)}, f32[3,1024]{1,0:T(4,128)}, u32[]{:S(2)}) copy-start(f32[3,1024]{1,0:T(4,128)} %param.10) | copy-start | bytes 36868
  17.6 350.4 %all-to-all-start = ((bf16[32,1024,256]{2,1,0:T(8,128)(2,1)}), bf16[32,1024,256]{2,1,0:T(8,128)(2,1)}, u32[]{:S(2)}, u32[]{:S(2)}) async-start(bf16[32,1024,256]{2,1,0:T(8,128)(2,1)} %stack.2), calls=%async_computation | async-start | bytes 33554432 | tf_op jit(solution)/shard_map/all_to_all | solution.py:48
  27.2 424.2 %all-reduce.5.cloned.1.call-start = ((), (), s32[]{:S(2)}) async-start(), calls=%async_computation.2 | async-start | bytes 2097152 | tf_op jit(solution)/shard_map/psum | solution.py:44
  366.9 1.0 copy-start.2
  367.9 224.6 %all-reduce.7.cloned.1.call-start = ((), (), s32[]{:S(2)}) async-start(), calls=%async_computation.3 | async-start | bytes 524288 | tf_op jit(solution)/shard_map/psum | solution.py:68
  449.5 5.8 copy-start.1
  451.3 247.0 %all-reduce.9.cloned.1.call-start = ((), (), s32[]{:S(2)}) async-start(), calls=%async_computation.4 | async-start | bytes 1048576 | tf_op jit(solution)/shard_map/psum | solution.py:67
  452.8 4.1 copy-start
Sparse Core Ops, SparseCore 0:
  10.8 210.5 all-gather.1
  368.0 42.2 all-reduce.4
  451.4 141.0 all-reduce.6
  596.2 102.0 all-reduce.8
